TPU v7x, 32 devices: a whole 2x2x4 slice. The times are simulated.
32 devices in a mesh: wide: 8 (over z, x), narrow: 4 (over y, core).
Axes of the slice: x: 2, y: 2, z: 4, core: 2. Of those that a mesh axis runs over, the one named last changes fastest.
Arguments:
- states: bfloat16 [256, 262144], P('narrow', 'wide'), may hold values from -6 to 6
- obs_ens: bfloat16 [256, 32768], P('narrow', 'wide'), may hold values from -6 to 6
- obs_value: float32 [32768], P('wide'), may hold values from -6 to 6
- obs_prec: float32 [32768], P('wide'), may hold values from 0.1 to 1
- obs_pick: int32 [32, 1024], P('wide'), may hold values from 0 to 4607, as said below
- taper: float32 [32, 1024], P(('wide', 'narrow')), may hold values from 0.1 to 1
Outputs:
- analysis: bfloat16 [256, 262144], P('narrow', 'wide')
Inputs may be any that keep to these rules, and one draw needn't show every extreme that they name: `obs_pick`: within a region the 1024 rows are distinct.
All inputs are finite; a program needn't handle non-finite values.
Results may differ from a plain program's by a relative error of at most 0.0057.
Values may be sent and summed in bfloat16 or wider, within the bound.
No kernel may reach another device: no remote copies, remote signals or barrier semaphores. Data moves between devices by JAX's collectives and lax.ppermute only.
A program may use at most 64 MiB of HBM per device.

v0:
```python
import jax
import jax.numpy as jnp
from jax import lax
from jax.sharding import PartitionSpec as P

HALO = 256
ITERS = 6


def padded(array, sides, width):
    for axis, dim in sides:
        size, length = (lax.axis_size(axis), array.shape[dim])
        up = [(i, (i + 1) % size) for i in range(size)]
        down = [(j, i) for i, j in up]
        last = lax.slice_in_dim(array, length - width, length, axis=dim)
        leading = lax.slice_in_dim(array, 0, width, axis=dim)
        before = lax.ppermute(last, axis, up)
        after = lax.ppermute(leading, axis, down)
        array = jnp.concatenate([before, array, after], axis=dim)
    return array


def analyse(ensemble, observed, precision, taper_row, regional):
    members = ensemble.shape[0]
    obs_mean = jnp.mean(ensemble, axis=0)
    obs_pert = ensemble - obs_mean
    obs_weight = precision * taper_row
    scaled = (obs_pert * jnp.sqrt(obs_weight)).astype(jnp.bfloat16)
    identity = jnp.eye(members, dtype=jnp.float32)
    gram_sum = lax.dot_general(
        scaled, scaled, (((1,), (1,)), ((), ())), preferred_element_type=jnp.float32
    )
    precision_matrix = gram_sum + (members - 1.0) * identity
    forcing = jnp.dot(
        obs_pert,
        obs_weight * (observed - obs_mean),
        precision=lax.Precision.HIGHEST,
        preferred_element_type=jnp.float32,
    )
    norm_scale = jnp.sqrt(jnp.sum(precision_matrix * precision_matrix))
    current = precision_matrix / norm_scale
    root_iter = identity
    for iteration in range(ITERS):
        middle = 1.5 * identity - 0.5 * jnp.dot(
            root_iter, current, precision=lax.Precision.HIGHEST, preferred_element_type=jnp.float32
        )
        current = jnp.dot(
            current, middle, precision=lax.Precision.HIGHEST, preferred_element_type=jnp.float32
        )
        root_iter = jnp.dot(
            middle, root_iter, precision=lax.Precision.HIGHEST, preferred_element_type=jnp.float32
        )
    inv_root = root_iter / jnp.sqrt(norm_scale)
    inner = jnp.dot(
        inv_root, forcing, precision=lax.Precision.HIGHEST, preferred_element_type=jnp.float32
    )
    mean_weights = jnp.dot(
        inv_root, inner, precision=lax.Precision.HIGHEST, preferred_element_type=jnp.float32
    )
    transform = (jnp.sqrt(members - 1.0) * inv_root + mean_weights[:, None]).astype(jnp.bfloat16)
    state_mean = jnp.mean(regional.astype(jnp.float32), axis=0)
    state_pert = (regional.astype(jnp.float32) - state_mean).astype(jnp.bfloat16)
    mixed = lax.dot_general(
        transform, state_pert, (((0,), (0,)), ((), ())), preferred_element_type=jnp.float32
    )
    return (state_mean + mixed).astype(jnp.bfloat16)


def body(states, obs_ens, obs_value, obs_prec, obs_pick, taper):
    band_regions = lax.axis_size("narrow")
    position = lax.axis_index("narrow")
    members = obs_ens.shape[0] * band_regions
    extended = padded(obs_ens, (("wide", 1),), HALO)
    stat_pair = padded(jnp.stack([obs_value, obs_prec]), (("wide", 1),), HALO)
    own_rows = lax.dynamic_index_in_dim(obs_pick, position, 0, keepdims=False)
    chosen = jnp.take(extended, obs_pick.reshape(-1), axis=1).reshape(
        extended.shape[0], band_regions, -1
    )
    arrived = lax.all_to_all(chosen, "narrow", split_axis=1, concat_axis=0, tiled=True)
    picked = arrived.reshape(members, -1)
    stat_rows = jnp.take(stat_pair, own_rows, axis=1)
    regional = lax.all_to_all(states, "narrow", split_axis=1, concat_axis=0, tiled=True)
    result = analyse(picked.astype(jnp.float32), stat_rows[0], stat_rows[1], taper[0], regional)
    return lax.all_to_all(result, "narrow", split_axis=0, concat_axis=1, tiled=True)


def solution(mesh):
    return jax.shard_map(
        body,
        mesh=mesh,
        in_specs=(
            P("narrow", "wide"),
            P("narrow", "wide"),
            P("wide"),
            P("wide"),
            P("wide", None),
            P(("wide", "narrow"), None),
        ),
        out_specs=P("narrow", "wide"),
        check_vma=False,
    )
```

profile of v0, /device:TPU:0, one launch (start us, length us, event | category | flops | bytes accessed | tf_op | source)
XLA Modules:
  0.0 160.5 jit_solution(12780005530070920755)
XLA Ops:
  0.0 0.7 pad_maximum_fusion.3
  0.7 3.0 %collective-permute-start.2 = (f32[2,256]{1,0:T(2,128)S(1)}, f32[2,256]{1,0:T(2,128)S(1)}, u32[]{:S(2)}, u32[]{:S(2)}) collective-permute-start(f32[2,256]{1,0:T(2,128)S(1)} %get-tuple-element.11), channel_id=1, source_target_pairs={{0,4},{4,8},{8,12},{12,16},{16,20},{20,24},{24,28},{28,0},{1,5},{5... | collective-permute-start | bytes 6152 | tf_op jit(solution)/shard_map/ppermute | solution.py:17
  3.7 3.1 %collective-permute-start.3 = (f32[2,256]{1,0:T(2,128)S(1)}, f32[2,256]{1,0:T(2,128)S(1)}, u32[]{:S(2)}, u32[]{:S(2)}) collective-permute-start(f32[2,256]{1,0:T(2,128)S(1)} %get-tuple-element.12), channel_id=1, source_target_pairs={{4,0},{8,4},{12,8},{16,12},{20,16},{24,20},{28,24},{0,28},{5,1},{9... | collective-permute-start | bytes 6152 | tf_op jit(solution)/shard_map/ppermute | solution.py:18
  6.9 1.5 copy.24
  8.4 0.1 collective-permute-start
  8.5 4.7 %collective-permute-start.1 = (bf16[64,256]{0,1:T(8,128)(2,1)S(1)}, bf16[64,256]{0,1:T(8,128)(2,1)S(1)}, u32[]{:S(2)}, u32[]{:S(2)}) collective-permute-start(bf16[64,256]{0,1:T(8,128)(2,1)S(1)} %get-tuple-element.10), channel_id=1, source_target_pairs={{4,0},{8,4},{12,8},{16,12},{20,16},{24,20},{28,24},{0,28},{5,1},{9... | collective-permute-start | bytes 98312 | tf_op jit(solution)/shard_map/ppermute | solution.py:18
  13.2 0.7 compare_and_fusion
  13.9 0.7 compare_select_fusion.2
  14.7 0.7 copy.34
  15.4 0.9 copy.29
  16.4 4.6 %copy.36 = bf16[8,4,8,8192]{3,2,0,1:T(8,128)(2,1)} copy(bf16[8,4,8,8192]{3,2,1,0:T(8,128)(2,1)} %bitcast.95) | data formatting | bytes 8388608 | tf_op jit(solution)/shard_map/all_to_all | solution.py:82
  21.0 0.0 collective-permute-done
  21.0 0.0 collective-permute-done.1
  21.0 0.2 pad_maximum_fusion
  21.2 0.0 copy-start
  21.3 0.0 copy-start.1
  21.3 12.1 %gather_fusion = bf16[4096,64]{1,0:T(8,128)(2,1)S(1)} fusion(bf16[64,4608]{0,1:T(8,128)(2,1)S(1)} %pad_maximum_fusion, s32[4096]{0:T(1024)S(1)} %broadcast_clamp_fusion), kind=kCustom, calls=%fused_computation | custom fusion | bytes 1064960 | tf_op jit(solution)/shard_map/jit(_take)/gather | solution.py:76
  33.4 0.3 copy.27
  33.7 0.8 broadcast_select_fusion
  34.6 3.5 %all-to-all-start.1 = ((bf16[64,4,1024]{2,0,1:T(8,128)(2,1)}), bf16[64,4,1024]{2,0,1:T(8,128)(2,1)S(1)}, u32[]{:S(2)}, u32[]{:S(2)}) async-start(bf16[64,4,1024]{2,0,1:T(8,128)(2,1)} %broadcast_select_fusion), calls=%async_computation.1 | async-start | bytes 1048576 | tf_op jit(solution)/shard_map/all_to_all | solution.py:79
  38.1 0.0 collective-permute-done.2
  38.1 0.0 collective-permute-done.3
  38.1 0.0 copy-done
  38.1 0.0 copy-done.1
  38.2 0.7 copy.28
  38.9 4.0 %gather_fusion.1 = f32[1024,2]{1,0:T(8,128)} fusion(f32[2,4608]{0,1:T(8,128)S(1)} %copy.28, s32[1024]{0:T(1024)S(1)} %broadcast_clamp_fusion.1), kind=kCustom, calls=%fused_computation.1 | custom fusion | bytes 20480 | tf_op jit(solution)/shard_map/jit(_take)/gather | solution.py:81
  42.9 1.2 select_bitcast_fusion
  44.2 2.7 %all-to-all-done.1 = bf16[64,4,1024]{2,0,1:T(8,128)(2,1)S(1)} async-done(((bf16[64,4,1024]{2,0,1:T(8,128)(2,1)}), bf16[64,4,1024]{2,0,1:T(8,128)(2,1)S(1)}, u32[]{:S(2)}, u32[]{:S(2)}) %all-to-all-start.1) | async-done | bytes 524320 | tf_op jit(solution)/shard_map/all_to_all | solution.py:79
  46.8 5.0 %all-to-all-start = ((bf16[64,4,8192]{2,0,1:T(8,128)(2,1)}), bf16[64,4,8192]{2,0,1:T(8,128)(2,1)}, u32[]{:S(2)}, u32[]{:S(2)}) async-start(bf16[64,4,8192]{2,0,1:T(8,128)(2,1)} %bitcast.92), calls=%async_computation | async-start | bytes 8388608 | tf_op jit(solution)/shard_map/all_to_all | solution.py:82
  51.9 0.1 convert_reduce_fusion.1
  52.0 0.2 copy.30
  52.2 0.6 fusion.11
  52.8 0.1 fusion.9
  52.9 1.0 multiply_reduce_fusion
  54.6 0.3 fusion.7
  54.9 0.4 fusion.15
  55.3 0.3 fusion.12
  55.6 0.4 fusion.6
  56.0 0.4 fusion.19
  56.4 0.4 fusion.18
  56.8 0.4 fusion.5
  57.1 0.4 fusion.21
  57.5 0.4 fusion.20
  57.9 0.4 fusion.4
  58.3 0.4 fusion.23
  58.7 0.4 fusion.22
  59.1 0.4 fusion.3
  59.5 0.4 fusion.24
  59.9 0.4 fusion.25
  60.2 0.4 fusion.2
  60.6 0.4 convolution_divide_fusion
  61.0 0.1 fusion.8
  61.2 0.9 convolution_bitcast_fusion
  62.1 0.3 convolution_bitcast_fusion.1
  62.4 0.3 fusion.26
  62.7 37.2 %all-to-all-done = bf16[64,4,8192]{2,0,1:T(8,128)(2,1)} async-done(((bf16[64,4,8192]{2,0,1:T(8,128)(2,1)}), bf16[64,4,8192]{2,0,1:T(8,128)(2,1)}, u32[]{:S(2)}, u32[]{:S(2)}) %all-to-all-start) | async-done | bytes 4194336 | tf_op jit(solution)/shard_map/all_to_all | solution.py:82
  99.9 2.9 %convert_reduce_fusion = f32[8192]{0:T(1024)S(1)} fusion(bf16[64,4,8192]{2,0,1:T(8,128)(2,1)} %all-to-all-done), kind=kLoop, calls=%fused_computation.7 | loop fusion | flops 4186112 | bytes 4227072 | tf_op jit(solution)/shard_map/reduce_sum | solution.py:61
  102.8 3.3 %fusion.1 = bf16[256,8192]{1,0:T(8,128)(2,1)S(1)} fusion(f32[8192]{0:T(1024)S(1)} %broadcast_multiply_fusion, bf16[64,4,8192]{2,0,1:T(8,128)(2,1)} %all-to-all-done), kind=kLoop, calls=%fused_computation.5 | loop fusion | flops 6291456 | bytes 8421376 | tf_op jit(solution)/shard_map/convert_element_type | solution.py:62
  106.2 1.4 fusion
  107.5 50.7 %all_to_all.41 = bf16[4,64,8192]{2,1,0:T(8,128)(2,1)S(1)} all-to-all(bf16[4,64,8192]{2,1,0:T(8,128)(2,1)S(1)} %bitcast.91), channel_id=1, replica_groups=mesh['wide'=8,'narrow'=4] {'narrow'}, dimensions={0} | all-to-all | bytes 8388608 | tf_op jit(solution)/shard_map/all_to_all | solution.py:84
  158.2 2.3 %copy.33 = bf16[4,8,8,8192]{3,2,0,1:T(8,128)(2,1)} copy(bf16[4,8,8,8192]{3,2,1,0:T(8,128)(2,1)S(1)} %bitcast.93) | data formatting | bytes 8388608 | tf_op jit(solution)/shard_map/all_to_all | solution.py:84
  (8 shorter events, 0.1 us)
Async XLA Ops:
  0.7 37.3 %collective-permute-start.2 = (f32[2,256]{1,0:T(2,128)S(1)}, f32[2,256]{1,0:T(2,128)S(1)}, u32[]{:S(2)}, u32[]{:S(2)}) collective-permute-start(f32[2,256]{1,0:T(2,128)S(1)} %get-tuple-element.11), channel_id=1, source_target_pairs={{0,4},{4,8},{8,12},{12,16},{16,20},{20,24},{24,28},{28,0},{1,5},{5... | collective-permute-start | bytes 6152 | tf_op jit(solution)/shard_map/ppermute | solution.py:17
  3.7 34.3 %collective-permute-start.3 = (f32[2,256]{1,0:T(2,128)S(1)}, f32[2,256]{1,0:T(2,128)S(1)}, u32[]{:S(2)}, u32[]{:S(2)}) collective-permute-start(f32[2,256]{1,0:T(2,128)S(1)} %get-tuple-element.12), channel_id=1, source_target_pairs={{4,0},{8,4},{12,8},{16,12},{20,16},{24,20},{28,24},{0,28},{5,1},{9... | collective-permute-start | bytes 6152 | tf_op jit(solution)/shard_map/ppermute | solution.py:18
  8.4 12.6 %collective-permute-start = (bf16[64,256]{0,1:T(8,128)(2,1)S(1)}, bf16[64,256]{0,1:T(8,128)(2,1)S(1)}, u32[]{:S(2)}, u32[]{:S(2)}) collective-permute-start(bf16[64,256]{0,1:T(8,128)(2,1)S(1)} %get-tuple-element.9), channel_id=1, source_target_pairs={{0,4},{4,8},{8,12},{12,16},{16,20},{20,24},{24,28},{28,0},{1,5},{5... | collective-permute-start | bytes 98312 | tf_op jit(solution)/shard_map/ppermute | solution.py:17
  8.5 12.5 %collective-permute-start.1 = (bf16[64,256]{0,1:T(8,128)(2,1)S(1)}, bf16[64,256]{0,1:T(8,128)(2,1)S(1)}, u32[]{:S(2)}, u32[]{:S(2)}) collective-permute-start(bf16[64,256]{0,1:T(8,128)(2,1)S(1)} %get-tuple-element.10), channel_id=1, source_target_pairs={{4,0},{8,4},{12,8},{16,12},{20,16},{24,20},{28,24},{0,28},{5,1},{9... | collective-permute-start | bytes 98312 | tf_op jit(solution)/shard_map/ppermute | solution.py:18
  21.2 16.8 %copy-start = (f32[4096]{0:T(1024)S(1)}, f32[4096]{0:T(1024)}, u32[]{:S(2)}) copy-start(f32[4096]{0:T(1024)} %param.9) | copy-start | bytes 49156
  21.3 16.8 %copy-start.1 = (f32[4096]{0:T(1024)S(1)}, f32[4096]{0:T(1024)}, u32[]{:S(2)}) copy-start(f32[4096]{0:T(1024)} %param.8) | copy-start | bytes 49156
  34.6 12.3 %all-to-all-start.1 = ((bf16[64,4,1024]{2,0,1:T(8,128)(2,1)}), bf16[64,4,1024]{2,0,1:T(8,128)(2,1)S(1)}, u32[]{:S(2)}, u32[]{:S(2)}) async-start(bf16[64,4,1024]{2,0,1:T(8,128)(2,1)} %broadcast_select_fusion), calls=%async_computation.1 | async-start | bytes 1048576 | tf_op jit(solution)/shard_map/all_to_all | solution.py:79
  46.8 53.1 %all-to-all-start = ((bf16[64,4,8192]{2,0,1:T(8,128)(2,1)}), bf16[64,4,8192]{2,0,1:T(8,128)(2,1)}, u32[]{:S(2)}, u32[]{:S(2)}) async-start(bf16[64,4,8192]{2,0,1:T(8,128)(2,1)} %bitcast.92), calls=%async_computation | async-start | bytes 8388608 | tf_op jit(solution)/shard_map/all_to_all | solution.py:82
where the time goes:
time: 161 us
  blocking collectives  50.7 us (31%)
  waiting for transfers between devices  39.9 us (25%)
  local copies, waits for them, and re-layouts  27.6 us (17%)
  starting transfers between devices  19.4 us (12%)
  other arithmetic  11.7 us (7%)
  matrix products  10.2 us (6%)
    all_to_all x1, blocking collectives, body(): lax.all_to_all(result, 'narrow', split_axis=0, concat_axis=1, tiled=True)  50.7 us
    all_to_all x1, waiting for transfers between devices, body(): lax.all_to_all(states, 'narrow', split_axis=1, concat_axis=0, tiled=True)  37.2 us
    gather x2, local copies, waits for them, and re-layouts, body(): jnp.take(extended, obs_pick.reshape(-1), axis=1)  12.5 us
    ppermute x2, starting transfers between devices, padded(): after = lax.ppermute(leading, axis, down)  7.81 us
    all_to_all x1, starting transfers between devices, body(): lax.all_to_all(states, 'narrow', split_axis=1, concat_axis=0, tiled=True)  5.04 us
    all_to_all x1, local copies, waits for them, and re-layouts, body(): lax.all_to_all(states, 'narrow', split_axis=1, concat_axis=0, tiled=True)  4.64 us
    gather x1, local copies, waits for them, and re-layouts, body(): stat_rows = jnp.take(stat_pair, own_rows, axis=1)  4.04 us
    all_to_all x1, starting transfers between devices, body(): lax.all_to_all(chosen, 'narrow', split_axis=1, concat_axis=0, tiled=True)  3.47 us
  transfers between devices with their start and end apart: 6, of which 2 were waited for; matrix products, arithmetic and copies ran while one was open for 24% of the time, Pallas kernels for 0%

commit v1 on v0

v1 whole, which is shorter than its diff:
```python
import functools

import jax
import jax.numpy as jnp
from jax import lax
from jax.experimental import pallas as pl
from jax.experimental.pallas import tpu as pltpu
from jax.sharding import PartitionSpec as P

HALO = 256
ITERS = 6
LANES = 128


VMEM = pl.BlockSpec(memory_space=pltpu.VMEM)
SMEM = pl.BlockSpec(memory_space=pltpu.SMEM)
HBM = pl.BlockSpec(memory_space=pltpu.HBM)


def params():
    return pltpu.CompilerParams(vmem_limit_bytes=16 << 20)


def cost(flops, moved):
    return pl.CostEstimate(flops=flops, bytes_accessed=moved, transcendentals=0)


def swap(array, d):
    n = lax.axis_size("narrow")
    return lax.ppermute(array, "narrow", [(i, i ^ d) for i in range(n)])


def halo(array, width, flip):
    size, n, length = lax.axis_size("wide"), lax.axis_size("narrow"), array.shape[1]
    up = [(w * n + i, (w + 1) % size * n + (i ^ flip)) for w in range(size) for i in range(n)]
    down = [(w * n + i, (w - 1) % size * n + (i ^ flip)) for w in range(size) for i in range(n)]
    before = lax.ppermute(array[:, length - width :], ("wide", "narrow"), up)
    after = lax.ppermute(array[:, :width], ("wide", "narrow"), down)
    return before, after


def pack_kernel(partners, cells, start, states_ref, *refs):
    count = len(partners)
    outs, sems = refs[:count], refs[count]
    pos = lax.axis_index("narrow")
    width = outs[0].shape[1]
    copies = []
    for k, d in enumerate(partners):
        column = pl.multiple_of((pos ^ d) * cells + start, LANES)
        copies.append(
            pltpu.make_async_copy(states_ref.at[:, pl.ds(column, width)], outs[k], sems.at[k])
        )
        copies[-1].start()
    for copy in copies:
        copy.wait()


def pack(states, partners, cells, start, width):
    rows = states.shape[0]
    count = len(partners)
    return pl.pallas_call(
        functools.partial(pack_kernel, partners, cells, start),
        in_specs=[HBM],
        out_specs=[VMEM] * count,
        out_shape=[jax.ShapeDtypeStruct((rows, width), jnp.bfloat16)] * count,
        scratch_shapes=[pltpu.SemaphoreType.DMA((count,))],
        compiler_params=params(),
        cost_estimate=cost(0, 4 * count * rows * width),
        name="pack",
    )(states)


def gather_kernel(pick_ref, *refs):
    parts, out_ref, table_ref, rows_ref = refs[:-3], refs[-3], refs[-2], refs[-1]
    base = 0
    for own_ref, other_ref in zip(parts[::2], parts[1::2]):
        for k in range(own_ref.shape[1] // LANES):
            block = jnp.concatenate(
                [
                    r[:, k * LANES : (k + 1) * LANES].astype(jnp.float32)
                    for r in (own_ref, other_ref)
                ],
                axis=0,
            )
            table_ref[base : base + LANES, :] = block.T
            base += LANES
    step = 16
    regions, used, _ = out_ref.shape
    pos = lax.axis_index("narrow")

    for region in range(regions):

        def move(g, carry):
            for u in range(step):
                j = g * step + u
                row = pick_ref[pos ^ (2 * region), j]
                rows_ref[pl.ds(j, 1), :] = table_ref[pl.ds(row, 1), :]
            return carry

        lax.fori_loop(0, used // step, move, 0)
        out_ref[region] = rows_ref[...].astype(jnp.bfloat16)


def gather(picks, parts):
    rows = parts[0].shape[0]
    window = sum(p.shape[1] for p in parts[::2])
    regions, used = picks.shape[0] // 2, picks.shape[1]
    return pl.pallas_call(
        gather_kernel,
        in_specs=[SMEM] + [VMEM] * len(parts),
        out_specs=VMEM,
        out_shape=jax.ShapeDtypeStruct((regions, used, 2 * rows), jnp.bfloat16),
        scratch_shapes=[
            pltpu.VMEM((window, 2 * rows), jnp.float32),
            pltpu.VMEM((used, 2 * rows), jnp.float32),
        ],
        compiler_params=params(),
        cost_estimate=cost(0, 16 * rows * (window + regions * used)),
        name="gather",
    )(picks, *parts)


def stats_kernel(pick_ref, taper_ref, *refs):
    parts, out_ref, table_ref = refs[:-2], refs[-2], refs[-1]
    base = 0
    for part in parts:
        for k in range(part.shape[1] // LANES):
            block = part[:, k * LANES : (k + 1) * LANES]
            block = jnp.concatenate([block, jnp.zeros((6, LANES), jnp.float32)], axis=0)
            table_ref[base : base + LANES, :] = block.T
            base += LANES
    step = 16
    used = out_ref.shape[0]
    pos = lax.axis_index("narrow")

    def move(g, carry):
        for u in range(step):
            j = g * step + u
            out_ref[pl.ds(j, 1), :] = table_ref[pl.ds(pick_ref[pos, j], 1), :]
        return carry

    lax.fori_loop(0, used // step, move, 0)
    for k in range(used // LANES):
        cut = slice(k * LANES, (k + 1) * LANES)
        column = jnp.broadcast_to(taper_ref[:, cut], (8, LANES)).T
        lane = lax.broadcasted_iota(jnp.int32, (LANES, 8), 1)
        out_ref[cut, :] = out_ref[cut, :] * jnp.where(lane == 1, column, 1.0)


def stats(picks, taper, parts):
    window = sum(p.shape[1] for p in parts)
    used = picks.shape[1]
    return pl.pallas_call(
        stats_kernel,
        in_specs=[SMEM] + [VMEM] * (1 + len(parts)),
        out_specs=VMEM,
        out_shape=jax.ShapeDtypeStruct((used, 8), jnp.float32),
        scratch_shapes=[pltpu.VMEM((window, 8), jnp.float32)],
        compiler_params=params(),
        cost_estimate=cost(0, 512 * (window + used)),
        name="stats",
    )(picks, taper, *parts)


def dot(a, b):
    return jnp.dot(a, b, precision=lax.Precision.HIGHEST, preferred_element_type=jnp.float32)


def transform_kernel(own_ref, stats_ref, *refs):
    others, out_ref = refs[:-1], refs[-1]
    ensemble = jnp.concatenate([own_ref[0]] + [r[...] for r in others], axis=1).astype(jnp.float32)
    members = ensemble.shape[1]
    value, weight = stats_ref[:, 0:1], stats_ref[:, 1:2]
    mean = jnp.sum(ensemble, axis=1, keepdims=True) * (1.0 / members)
    pert = ensemble - mean
    scaled = (pert * jnp.sqrt(weight)).astype(jnp.bfloat16)
    forcing = jnp.sum(pert * (weight * (value - mean)), axis=0, keepdims=True)
    row = lax.broadcasted_iota(jnp.int32, (members, members), 0)
    column = lax.broadcasted_iota(jnp.int32, (members, members), 1)
    identity = jnp.where(row == column, 1.0, 0.0)
    matrix = (members - 1.0) * identity + lax.dot_general(
        scaled, scaled, (((0,), (0,)), ((), ())), preferred_element_type=jnp.float32
    )
    squares = jnp.sum(jnp.sum(matrix * matrix, axis=0, keepdims=True), axis=1, keepdims=True)
    norm_scale = jnp.sqrt(squares)
    current = matrix / norm_scale
    root = 1.5 * identity - 0.5 * current
    current = dot(current, root)
    for iteration in range(1, ITERS):
        middle = 1.5 * identity - 0.5 * dot(root, current)
        if iteration < ITERS - 1:
            current = dot(current, middle)
        root = dot(middle, root)
    inv_root = root / jnp.sqrt(norm_scale)
    forcing = jnp.broadcast_to(forcing, (8, members))
    mean_weights = dot(dot(forcing, inv_root), inv_root)[0:1]
    out_ref[...] = (jnp.sqrt(jnp.float32(members - 1)) * inv_root + mean_weights).astype(jnp.bfloat16)


def transform(picked, stat, others):
    _, used, pair = picked.shape
    members = pair * (1 + len(others))
    return pl.pallas_call(
        transform_kernel,
        grid=(1,),
        in_specs=[
            pl.BlockSpec((1, used, pair), lambda i: (0, 0, 0)),
            pl.BlockSpec((used, 8), lambda i: (0, 0)),
        ]
        + [pl.BlockSpec((used, pair), lambda i: (0, 0))] * len(others),
        out_specs=pl.BlockSpec((members, members), lambda i: (0, 0)),
        out_shape=jax.ShapeDtypeStruct((members, members), jnp.bfloat16),
        compiler_params=params(),
        cost_estimate=cost(16 * 6 * 2 * members**3, 4 * used * members),
        name="transform",
    )(picked, stat, *others)


def apply_kernel(parts, at_ref, weights_ref, *refs):
    del at_ref
    sources, outs = refs[:parts], refs[-parts:]
    pieces = [r[...].astype(jnp.float32) for r in sources]
    rows = pieces[0].shape[0]
    total = sum(jnp.sum(p, axis=0, keepdims=True) for p in pieces)
    mean = total * (1.0 / (rows * parts))
    pert = jnp.concatenate([(p - mean).astype(jnp.bfloat16) for p in pieces], axis=0)
    mixed = jnp.dot(weights_ref[...], pert, preferred_element_type=jnp.float32)
    result = (mixed + mean).astype(jnp.bfloat16)
    for d in range(parts):
        outs[d][...] = result[d * rows : (d + 1) * rows]


def apply(weights, states, arrived, result, at, block):
    rows, width = arrived[0].shape
    parts = len(arrived) + 1
    members = rows * parts
    near = pl.BlockSpec((rows, block), lambda i, at: (0, at[0] + i))
    far = pl.BlockSpec((rows, block), lambda i, at: (0, i))
    given = [] if result is None else [result]
    return pl.pallas_call(
        functools.partial(apply_kernel, parts),
        grid_spec=pltpu.PrefetchScalarGridSpec(
            num_scalar_prefetch=1,
            grid=(width // block,),
            in_specs=[pl.BlockSpec((members, members), lambda i, at: (0, 0)), near]
            + [far] * (parts - 1)
            + [HBM] * len(given),
            out_specs=[near] + [far] * (parts - 1),
        ),
        out_shape=[jax.ShapeDtypeStruct(states.shape, jnp.bfloat16)]
        + [jax.ShapeDtypeStruct((rows, width), jnp.bfloat16)] * (parts - 1),
        input_output_aliases={2 + parts: 0} if given else {},
        compiler_params=params(),
        cost_estimate=cost(2 * members * members * width, 4 * members * width),
        name="apply",
    )(at, weights, states, *arrived, *given)


def place_kernel(cells, start, result_ref, *refs):
    del result_ref
    parts, out_ref, sems = refs[:-2], refs[-2], refs[-1]
    pos = lax.axis_index("narrow")
    copies = []
    for k, part in enumerate(parts):
        column = pl.multiple_of((pos ^ (k + 1)) * cells + start, LANES)
        copies.append(
            pltpu.make_async_copy(part, out_ref.at[:, pl.ds(column, part.shape[1])], sems.at[k])
        )
        copies[-1].start()
    for copy in copies:
        copy.wait()


def place(result, parts, cells, start):
    return pl.pallas_call(
        functools.partial(place_kernel, cells, start),
        in_specs=[HBM] + [VMEM] * len(parts),
        out_specs=HBM,
        out_shape=jax.ShapeDtypeStruct(result.shape, result.dtype),
        scratch_shapes=[pltpu.SemaphoreType.DMA((len(parts),))],
        input_output_aliases={0: 0},
        compiler_params=params(),
        cost_estimate=cost(0, sum(4 * p.size for p in parts)),
        name="place",
    )(result, *parts)


def body(states, obs_ens, obs_value, obs_prec, obs_pick, taper):
    n = lax.axis_size("narrow")
    pos = lax.axis_index("narrow")
    cells = states.shape[1] // n
    unit = cells // 8
    chunks = [(0, 4 * unit), (4 * unit, 2 * unit), (6 * unit, 2 * unit)]

    def send(source, partners, k):
        moved = []
        for d, part in zip(partners, pack(source, partners, cells, *chunks[k])):
            moved.append(swap(part, d))
        return moved

    far = list(range(2, n))
    incoming = [send(states, far, 0)]

    other = swap(obs_ens, 1)
    before, after = halo(obs_ens, HALO, 0)
    other_before, other_after = halo(obs_ens, HALO, 1)
    marks = jnp.stack([obs_value, obs_prec])
    mark_before, mark_after = halo(marks, HALO, 0)
    incoming[0] = send(states, [1], 0) + incoming[0]
    picked = gather(obs_pick, [before, other_before, obs_ens, other, after, other_after])
    states_late, picked = lax.optimization_barrier((states, picked))
    others = []
    for d in far[::2]:
        others.append(swap(picked[d // 2], d))
    for k in range(1, len(chunks)):
        moved = send(states_late, far, k)
        incoming.append(send(states_late, [1], k) + moved)

    weights = transform(picked, stats(obs_pick, taper, [mark_before, marks, mark_after]), others)

    result, outgoing = None, []
    for k, (start, width) in enumerate(chunks):
        at = jnp.reshape((pos * cells + start) // unit, (1,))
        result, *leaving = apply(weights, states, incoming[k], result, at, unit)
        moved = []
        for d, part in enumerate(leaving, 1):
            moved.append(swap(part, d))
        outgoing.append(moved)
    for (start, _), moved in zip(chunks, outgoing):
        result = place(result, moved, cells, start)
    return result


def solution(mesh):
    return jax.shard_map(
        body,
        mesh=mesh,
        in_specs=(
            P("narrow", "wide"),
            P("narrow", "wide"),
            P("wide"),
            P("wide"),
            P("wide", None),
            P(("wide", "narrow"), None),
        ),
        out_specs=P("narrow", "wide"),
        check_vma=False,
    )
```

time: 161 us -> 118 us (0.73)
  blocking collectives: 50.7 us -> 0 us
  Pallas kernels: 0 us -> 31.2 us
  local copies, waits for them, and re-layouts: 27.6 us -> 15.9 us
  other arithmetic: 11.7 us -> 0.77 us
  matrix products: 10.2 us -> 0 us
  starting transfers between devices: 19.4 us -> 27.5 us
  waiting for transfers between devices: 39.9 us -> 41.7 us
    all_to_all x1 -> x0, blocking collectives: 50.7 us -> none  [body(): lax.all_to_all(result, 'narrow', split_axis=0, concat_axis=1, tiled=True)]
    ppermute x4 -> x26, waiting for transfers between devices: 0.01 us -> 41.7 us  [the longest x20 41.7 us: swap(): return lax.ppermute(array, 'narrow', [(i, i ^ d) for i in range(n)])]
    all_to_all x2 -> x0, waiting for transfers between devices: 39.9 us -> none  [the longest x1 37.2 us: body(): lax.all_to_all(states, 'narrow', split_axis=1, concat_axis=0, tiled=True)]
    pallas_call x0 -> x15, Pallas kernels: none -> 31.2 us  [the longest x1 8.54 us: transform(): pl.pallas_call(transform_kernel, grid=(1,), in_specs=[pl.BlockSpec((1, us...]
    ppermute x4 -> x26, starting transfers between devices: 10.9 us -> 27.5 us  [the longest x20 15.6 us: swap(): return lax.ppermute(array, 'narrow', [(i, i ^ d) for i in range(n)])]
    gather x3 -> x0, local copies, waits for them, and re-layouts: 16.5 us -> none  [the longest x2 12.5 us: body(): jnp.take(extended, obs_pick.reshape(-1), axis=1)]
    unnamed x7 -> x36, local copies, waits for them, and re-layouts: 3.17 us -> 14.4 us
    dot_general x22 -> x0, matrix products: 10.2 us -> none  [the longest x6 2.22 us: analyse(): jnp.dot(root_iter, current, precision=lax.Precision.HIGHEST, preferred_el...]
  transfers between devices with their start and end apart: 6 -> 26, of which waited for: 2 -> 7; matrix products, arithmetic and copies ran while one was open for 24% -> 2% of each run, Pallas kernels for 0% -> 26%
where the time goes in v1:
time: 118 us; the launch traced here: 117 us
  waiting for transfers between devices  41.7 us (35%)
  Pallas kernels  31.2 us (26%)
  starting transfers between devices  27.5 us (23%)
  local copies, waits for them, and re-layouts  15.9 us (13%)
    ppermute x20, waiting for transfers between devices, swap(): return lax.ppermute(array, 'narrow', [(i, i ^ d) for i in range(n)])  41.7 us
    ppermute x20, starting transfers between devices, swap(): return lax.ppermute(array, 'narrow', [(i, i ^ d) for i in range(n)])  15.6 us
    unnamed x36, local copies, waits for them, and re-layouts  14.4 us
    pallas_call x1, Pallas kernels, transform(): pl.pallas_call(transform_kernel, grid=(1,), in_specs=[pl.BlockSpec((1, us...  8.54 us
    pallas_call x1, Pallas kernels, gather(): pl.pallas_call(gather_kernel, in_specs=[SMEM] + [VMEM] * len(parts), out_...  6.88 us
    ppermute x3, starting transfers between devices, halo(): after = lax.ppermute(array[:, :width], ('wide', 'narrow'), down)  6.39 us
    pallas_call x3, Pallas kernels, apply(): pl.pallas_call(functools.partial(apply_kernel, parts), grid_spec=pltpu.Pr...  6.38 us
    ppermute x3, starting transfers between devices, halo(): before = lax.ppermute(array[:, length - width:], ('wide', 'narrow'), up)  5.48 us
  transfers between devices with their start and end apart: 26, of which 7 were waited for; matrix products, arithmetic and copies ran while one was open for 2% of the time, Pallas kernels for 26%

profile of v1, /device:TPU:0, one launch (start us, length us, event | category | flops | bytes accessed | tf_op | source)
XLA Modules:
  0.0 117.3 jit_solution(5383807710850742480)
XLA Ops:
  0.0 0.5 collective-permute-start.2
  0.5 0.8 fusion.2
  1.3 2.5 %collective-permute-start = (bf16[64,256]{1,0:T(8,128)(2,1)S(1)}, bf16[64,256]{1,0:T(8,128)(2,1)S(1)}, u32[]{:S(2)}, u32[]{:S(2)}) collective-permute-start(bf16[64,256]{1,0:T(8,128)(2,1)S(1)} %get-tuple-element.46), channel_id=1, source_target_pairs={{0,4},{1,5},{2,6},{3,7},{4,8},{5,9},{6,10},{7,11},{8,12},{9,13},{1... | collective-permute-start | bytes 98312 | tf_op jit(solution)/shard_map/ppermute | solution.py:37
  3.8 1.4 %collective-permute-start.1 = (bf16[64,256]{1,0:T(8,128)(2,1)S(1)}, bf16[64,256]{1,0:T(8,128)(2,1)S(1)}, u32[]{:S(2)}, u32[]{:S(2)}) collective-permute-start(bf16[64,256]{1,0:T(8,128)(2,1)S(1)} %get-tuple-element.46), channel_id=1, source_target_pairs={{0,5},{1,4},{2,7},{3,6},{4,9},{5,8},{6,11},{7,10},{8,13},{9,12},{1... | collective-permute-start | bytes 98312 | tf_op jit(solution)/shard_map/ppermute | solution.py:37
  5.1 3.2 %collective-permute-start.3 = (bf16[64,256]{1,0:T(8,128)(2,1)S(1)}, bf16[64,256]{1,0:T(8,128)(2,1)S(1)}, u32[]{:S(2)}, u32[]{:S(2)}) collective-permute-start(bf16[64,256]{1,0:T(8,128)(2,1)S(1)} %get-tuple-element.45), channel_id=1, source_target_pairs={{0,28},{1,29},{2,30},{3,31},{4,0},{5,1},{6,2},{7,3},{8,4},{9,5},{1... | collective-permute-start | bytes 98312 | tf_op jit(solution)/shard_map/ppermute | solution.py:38
  8.3 0.1 collective-permute-start.4
  8.4 0.7 fusion.1
  9.1 2.2 %copy-done = bf16[64,32768]{1,0:T(8,128)(2,1)S(1)} copy-done((bf16[64,32768]{1,0:T(8,128)(2,1)S(1)}, bf16[64,32768]{1,0:T(8,128)(2,1)}, u32[]{:S(2)}) %copy-start) | copy-done | bytes 4194328
  11.3 0.9 pack.11
  12.2 0.0 copy-start.16
  12.2 0.0 copy-start.17
  12.2 0.0 copy-start.12
  12.2 0.1 pack.10
  12.3 0.0 collective-permute-done.refs_0_
  12.3 1.6 %collective-permute-start.5 = (f32[2,256]{1,0:T(2,128)S(1)}, f32[2,256]{1,0:T(2,128)S(1)}, u32[]{:S(2)}, u32[]{:S(2)}) collective-permute-start(f32[2,256]{1,0:T(2,128)S(1)} %get-tuple-element.48), channel_id=1, source_target_pairs={{0,4},{1,5},{2,6},{3,7},{4,8},{5,9},{6,10},{7,11},{8,12},{9,13},{1... | collective-permute-start | bytes 6152 | tf_op jit(solution)/shard_map/ppermute | solution.py:37
  13.9 0.0 collective-permute-done.1.refs_1_
  13.9 3.2 %collective-permute-start.6 = (f32[2,256]{1,0:T(2,128)S(1)}, f32[2,256]{1,0:T(2,128)S(1)}, u32[]{:S(2)}, u32[]{:S(2)}) collective-permute-start(f32[2,256]{1,0:T(2,128)S(1)} %get-tuple-element.47), channel_id=1, source_target_pairs={{0,28},{1,29},{2,30},{3,31},{4,0},{5,1},{6,2},{7,3},{8,4},{9,5},{1... | collective-permute-start | bytes 6152 | tf_op jit(solution)/shard_map/ppermute | solution.py:38
  17.1 1.6 %collective-permute-start.15 = (bf16[64,4096]{1,0:T(8,128)(2,1)}, bf16[64,4096]{1,0:T(8,128)(2,1)S(1)}, u32[]{:S(2)}, u32[]{:S(2)}) collective-permute-start(bf16[64,4096]{1,0:T(8,128)(2,1)} %get-tuple-element.31), channel_id=1, source_target_pairs={{0,2},{1,3},{2,0},{3,1},{4,6},{5,7},{6,4},{7,5},{8,10},{9,11},{10,... | collective-permute-start | bytes 1572872 | tf_op jit(solution)/shard_map/ppermute | solution.py:30
  18.7 0.0 collective-permute-done.2.refs_3_
  18.7 0.5 collective-permute-start.14
  19.2 6.9 %gather.1.own_ref = bf16[2,1024,128]{2,1,0:T(8,128)(2,1)S(1)} custom-call(s32[4,1024]{1,0:T(4,128)S(1)} %copy-done.11, bf16[64,256]{1,0:T(8,128)(2,1)S(1)} %collective-permute-done.refs_0_, bf16[64,256]{1,0:T(8,128)(2,1)S(1)} %collective-permute-done.1.refs_1_, bf16[64,4096]{1,0:T(8,128)(2,1)S(1)} %copy-done.6, ...), custom_call_target="tpu_custom_call" | custom-call | bytes 6815744 | tf_op jit(solution)/shard_map/gather/pallas_call | solution.py:108
  26.1 0.7 slice_bitcast_fusion
  26.9 1.6 %collective-permute-start.7 = (bf16[1024,128]{1,0:T(8,128)(2,1)}, bf16[1024,128]{1,0:T(8,128)(2,1)}, u32[]{:S(2)}, u32[]{:S(2)}) collective-permute-start(bf16[1024,128]{1,0:T(8,128)(2,1)} %slice_bitcast_fusion), channel_id=1, source_target_pairs={{0,2},{1,3},{2,0},{3,1},{4,6},{5,7},{6,4},{7,5},{8,10},{9,11},{10,... | collective-permute-start | bytes 786440 | tf_op jit(solution)/shard_map/ppermute | solution.py:30
  28.5 4.5 %stats.1.stats_ref = f32[1024,8]{1,0:T(8,128)S(1)} custom-call(s32[4,1024]{1,0:T(4,128)S(1)} %copy-done.11, f32[1,1024]{1,0:T(1,128)S(1)} %copy-done.12, f32[2,256]{1,0:T(2,128)S(1)} %collective-permute-done.5.refs_0_, f32[2,4096]{1,0:T(2,128)S(1)} %pad_maximum_fusion.refs_1_, f32[2,256]{1,0:T(2,128)S(1)} %collective-permute-done.6.refs_2_), custom_call_target="tpu_custom_call" | custom-call | bytes 2883584 | tf_op jit(solution)/shard_map/stats/pallas_call | solution.py:153
  33.0 0.0 copy-start.1
  33.0 2.2 %copy-done.1 = bf16[64,32768]{1,0:T(8,128)(2,1)S(1)} copy-done((bf16[64,32768]{1,0:T(8,128)(2,1)S(1)}, bf16[64,32768]{1,0:T(8,128)(2,1)}, u32[]{:S(2)}) %copy-start.1) | copy-done | bytes 4194328
  35.2 0.1 pack.9
  35.3 0.9 pack.7
  36.2 0.5 collective-permute-start.12
  36.7 0.7 collective-permute-start.13
  37.3 11.7 %collective-permute-done.7.refs_0_ = bf16[1024,128]{1,0:T(8,128)(2,1)} collective-permute-done((bf16[1024,128]{1,0:T(8,128)(2,1)}, bf16[1024,128]{1,0:T(8,128)(2,1)}, u32[]{:S(2)}, u32[]{:S(2)}) %collective-permute-start.7) | collective-permute-done | bytes 262176 | tf_op jit(solution)/shard_map/ppermute | solution.py:30
  49.1 8.5 %transform.1.weights_ref = bf16[256,256]{1,0:T(8,128)(2,1)S(1)} custom-call(bf16[2,1024,128]{2,1,0:T(8,128)(2,1)S(1)} %gather.1.own_ref, f32[1024,8]{1,0:T(8,128)S(1)} %stats.1.stats_ref, bf16[1024,128]{1,0:T(8,128)(2,1)} %collective-permute-done.7.refs_0_), custom_call_target="tpu_custom_call" | custom-call | flops 3221225472 | bytes 1048576 | tf_op jit(solution)/shard_map/transform/pallas_call | solution.py:203
  57.6 1.8 %collective-permute-start.10 = (bf16[64,2048]{1,0:T(8,128)(2,1)}, bf16[64,2048]{1,0:T(8,128)(2,1)S(1)}, u32[]{:S(2)}, u32[]{:S(2)}) collective-permute-start(bf16[64,2048]{1,0:T(8,128)(2,1)} %get-tuple-element.28), channel_id=1, source_target_pairs={{0,3},{1,2},{2,1},{3,0},{4,7},{5,6},{6,5},{7,4},{8,11},{9,10},{10,... | collective-permute-start | bytes 786440 | tf_op jit(solution)/shard_map/ppermute | solution.py:30
  59.4 0.4 collective-permute-start.9
  59.8 3.0 %apply.3 = (bf16[64,32768]{1,0:T(8,128)(2,1)}, bf16[64,4096]{1,0:T(8,128)(2,1)}, bf16[64,4096]{1,0:T(8,128)(2,1)}, bf16[64,4096]{1,0:T(8,128)(2,1)}) custom-call(s32[1]{0:T(128)} %bitcast.5.at_ref, bf16[256,256]{1,0:T(8,128)(2,1)S(1)} %transform.1.weights_ref, bf16[64,32768]{1,0:T(8,128)(2,1)S(1)} %copy-done.2, ...), custom_call_target="tpu_custom_call" | custom-call | flops 536870912 | bytes 4194304 | tf_op jit(solution)/shard_map/apply/pallas_call | solution.py:240
  62.8 0.0 collective-permute-done.13.refs_3_
  62.9 0.7 copy-done.7
  63.5 1.6 %collective-permute-start.18 = (bf16[64,4096]{1,0:T(8,128)(2,1)}, bf16[64,4096]{1,0:T(8,128)(2,1)S(1)}, u32[]{:S(2)}, u32[]{:S(2)}) collective-permute-start(bf16[64,4096]{1,0:T(8,128)(2,1)} %get-tuple-element.37), channel_id=1, source_target_pairs={{0,2},{1,3},{2,0},{3,1},{4,6},{5,7},{6,4},{7,5},{8,10},{9,11},{10,... | collective-permute-start | bytes 1572872 | tf_op jit(solution)/shard_map/ppermute | solution.py:30
  65.1 0.7 copy-done.9
  65.9 0.3 collective-permute-start.19
  66.1 2.2 %copy-done.3 = bf16[64,32768]{1,0:T(8,128)(2,1)S(1)} copy-done((bf16[64,32768]{1,0:T(8,128)(2,1)S(1)}, bf16[64,32768]{1,0:T(8,128)(2,1)}, u32[]{:S(2)}) %copy-start.3) | copy-done | bytes 4194328
  68.4 0.4 collective-permute-start.8
  68.7 0.5 copy-done.8
  69.3 0.1 copy-done.10
  69.3 2.2 %copy-done.4 = bf16[64,32768]{1,0:T(8,128)(2,1)S(1)} copy-done((bf16[64,32768]{1,0:T(8,128)(2,1)S(1)}, bf16[64,32768]{1,0:T(8,128)(2,1)}, u32[]{:S(2)}) %copy-start.4) | copy-done | bytes 4194328
  71.5 1.7 %apply.4 = (bf16[64,32768]{1,0:T(8,128)(2,1)}, bf16[64,2048]{1,0:T(8,128)(2,1)}, bf16[64,2048]{1,0:T(8,128)(2,1)S(1)}, bf16[64,2048]{1,0:T(8,128)(2,1)S(1)}) custom-call(s32[1]{0:T(128)} %bitcast.4.at_ref, bf16[256,256]{1,0:T(8,128)(2,1)S(1)} %transform.1.weights_ref, bf16[64,32768]{1,0:T(8,128)(2,1)S(1)} %copy-done.4, ...), custom_call_target="tpu_custom_call", output_to_operand_aliasing={{0}: (6, {})} | custom-call | flops 268435456 | bytes 2097152 | tf_op jit(solution)/shard_map/apply/pallas_call | solution.py:240
  73.3 0.7 copy-done.13
  73.9 0.7 copy-done.15
  74.6 0.3 collective-permute-start.20
  74.9 1.6 %collective-permute-start.21 = (bf16[64,2048]{1,0:T(8,128)(2,1)}, bf16[64,2048]{1,0:T(8,128)(2,1)S(1)}, u32[]{:S(2)}, u32[]{:S(2)}) collective-permute-start(bf16[64,2048]{1,0:T(8,128)(2,1)} %copy-done.15), channel_id=1, source_target_pairs={{0,2},{1,3},{2,0},{3,1},{4,6},{5,7},{6,4},{7,5},{8,10},{9,11},{10,... | collective-permute-start | bytes 786440 | tf_op jit(solution)/shard_map/ppermute | solution.py:30
  76.5 2.2 %copy-done.5 = bf16[64,32768]{1,0:T(8,128)(2,1)S(1)} copy-done((bf16[64,32768]{1,0:T(8,128)(2,1)S(1)}, bf16[64,32768]{1,0:T(8,128)(2,1)}, u32[]{:S(2)}) %copy-start.5) | copy-done | bytes 4194328
  78.7 1.6 %apply.5 = (bf16[64,32768]{1,0:T(8,128)(2,1)}, bf16[64,2048]{1,0:T(8,128)(2,1)S(1)}, bf16[64,2048]{1,0:T(8,128)(2,1)S(1)}, bf16[64,2048]{1,0:T(8,128)(2,1)S(1)}) custom-call(s32[1]{0:T(128)} %bitcast.at_ref, bf16[256,256]{1,0:T(8,128)(2,1)S(1)} %transform.1.weights_ref, bf16[64,32768]{1,0:T(8,128)(2,1)S(1)} %copy-done.5, ...), custom_call_target="tpu_custom_call", output_to_operand_aliasing={{0}: (6, {})} | custom-call | flops 268435456 | bytes 2097152 | tf_op jit(solution)/shard_map/apply/pallas_call | solution.py:240
  80.4 0.5 collective-permute-start.23
  80.9 3.1 %collective-permute-done.18.refs_1_ = bf16[64,4096]{1,0:T(8,128)(2,1)S(1)} collective-permute-done((bf16[64,4096]{1,0:T(8,128)(2,1)}, bf16[64,4096]{1,0:T(8,128)(2,1)S(1)}, u32[]{:S(2)}, u32[]{:S(2)}) %collective-permute-start.18) | collective-permute-done | bytes 524320 | tf_op jit(solution)/shard_map/ppermute | solution.py:30
  84.0 1.6 %collective-permute-start.24 = (bf16[64,2048]{1,0:T(8,128)(2,1)S(1)}, bf16[64,2048]{1,0:T(8,128)(2,1)S(1)}, u32[]{:S(2)}, u32[]{:S(2)}) collective-permute-start(bf16[64,2048]{1,0:T(8,128)(2,1)S(1)} %get-tuple-element.43), channel_id=1, source_target_pairs={{0,2},{1,3},{2,0},{3,1},{4,6},{5,7},{6,4},{7,5},{8,10},{9,11},{10,... | collective-permute-start | bytes 786440 | tf_op jit(solution)/shard_map/ppermute | solution.py:30
  85.6 8.9 %collective-permute-done.19.refs_2_ = bf16[64,4096]{1,0:T(8,128)(2,1)S(1)} collective-permute-done((bf16[64,4096]{1,0:T(8,128)(2,1)}, bf16[64,4096]{1,0:T(8,128)(2,1)S(1)}, u32[]{:S(2)}, u32[]{:S(2)}) %collective-permute-start.19) | collective-permute-done | bytes 524320 | tf_op jit(solution)/shard_map/ppermute | solution.py:30
  94.5 1.8 %collective-permute-start.25 = (bf16[64,2048]{1,0:T(8,128)(2,1)S(1)}, bf16[64,2048]{1,0:T(8,128)(2,1)S(1)}, u32[]{:S(2)}, u32[]{:S(2)}) collective-permute-start(bf16[64,2048]{1,0:T(8,128)(2,1)S(1)} %get-tuple-element.44), channel_id=1, source_target_pairs={{0,3},{1,2},{2,1},{3,0},{4,7},{5,6},{6,5},{7,4},{8,11},{9,10},{10,... | collective-permute-start | bytes 786440 | tf_op jit(solution)/shard_map/ppermute | solution.py:30
  96.3 1.2 place.3.result_ref
  97.5 3.4 %collective-permute-done.21.refs_1_ = bf16[64,2048]{1,0:T(8,128)(2,1)S(1)} collective-permute-done((bf16[64,2048]{1,0:T(8,128)(2,1)}, bf16[64,2048]{1,0:T(8,128)(2,1)S(1)}, u32[]{:S(2)}, u32[]{:S(2)}) %collective-permute-start.21) | collective-permute-done | bytes 262176 | tf_op jit(solution)/shard_map/ppermute | solution.py:30
  100.9 4.7 %collective-permute-done.22.refs_2_ = bf16[64,2048]{1,0:T(8,128)(2,1)S(1)} collective-permute-done((bf16[64,2048]{1,0:T(8,128)(2,1)S(1)}, bf16[64,2048]{1,0:T(8,128)(2,1)S(1)}, u32[]{:S(2)}, u32[]{:S(2)}) %collective-permute-start.22) | collective-permute-done | bytes 262176 | tf_op jit(solution)/shard_map/ppermute | solution.py:30
  105.6 0.9 place.4.result_ref
  106.5 5.6 %collective-permute-done.24.refs_1_ = bf16[64,2048]{1,0:T(8,128)(2,1)S(1)} collective-permute-done((bf16[64,2048]{1,0:T(8,128)(2,1)S(1)}, bf16[64,2048]{1,0:T(8,128)(2,1)S(1)}, u32[]{:S(2)}, u32[]{:S(2)}) %collective-permute-start.24) | collective-permute-done | bytes 262176 | tf_op jit(solution)/shard_map/ppermute | solution.py:30
  112.1 4.2 %collective-permute-done.25.refs_2_ = bf16[64,2048]{1,0:T(8,128)(2,1)S(1)} collective-permute-done((bf16[64,2048]{1,0:T(8,128)(2,1)S(1)}, bf16[64,2048]{1,0:T(8,128)(2,1)S(1)}, u32[]{:S(2)}, u32[]{:S(2)}) %collective-permute-start.25) | collective-permute-done | bytes 262176 | tf_op jit(solution)/shard_map/ppermute | solution.py:30
  116.4 0.9 place.5
  (43 shorter events, 0.2 us)
Async XLA Ops:
  0.0 18.7 %collective-permute-start.2 = (bf16[64,4096]{1,0:T(8,128)(2,1)}, bf16[64,4096]{1,0:T(8,128)(2,1)S(1)}, u32[]{:S(2)}, u32[]{:S(2)}) collective-permute-start(bf16[64,4096]{1,0:T(8,128)(2,1)} %refs_2_.1), channel_id=1, source_target_pairs={{0,1},{1,0},{2,3},{3,2},{4,5},{5,4},{6,7},{7,6},{8,9},{9,8},{10,11... | collective-permute-start | bytes 1572872 | tf_op jit(solution)/shard_map/ppermute | solution.py:30
  1.3 11.0 %collective-permute-start = (bf16[64,256]{1,0:T(8,128)(2,1)S(1)}, bf16[64,256]{1,0:T(8,128)(2,1)S(1)}, u32[]{:S(2)}, u32[]{:S(2)}) collective-permute-start(bf16[64,256]{1,0:T(8,128)(2,1)S(1)} %get-tuple-element.46), channel_id=1, source_target_pairs={{0,4},{1,5},{2,6},{3,7},{4,8},{5,9},{6,10},{7,11},{8,12},{9,13},{1... | collective-permute-start | bytes 98312 | tf_op jit(solution)/shard_map/ppermute | solution.py:37
  3.8 10.2 %collective-permute-start.1 = (bf16[64,256]{1,0:T(8,128)(2,1)S(1)}, bf16[64,256]{1,0:T(8,128)(2,1)S(1)}, u32[]{:S(2)}, u32[]{:S(2)}) collective-permute-start(bf16[64,256]{1,0:T(8,128)(2,1)S(1)} %get-tuple-element.46), channel_id=1, source_target_pairs={{0,5},{1,4},{2,7},{3,6},{4,9},{5,8},{6,11},{7,10},{8,13},{9,12},{1... | collective-permute-start | bytes 98312 | tf_op jit(solution)/shard_map/ppermute | solution.py:37
  5.1 12.0 %collective-permute-start.3 = (bf16[64,256]{1,0:T(8,128)(2,1)S(1)}, bf16[64,256]{1,0:T(8,128)(2,1)S(1)}, u32[]{:S(2)}, u32[]{:S(2)}) collective-permute-start(bf16[64,256]{1,0:T(8,128)(2,1)S(1)} %get-tuple-element.45), channel_id=1, source_target_pairs={{0,28},{1,29},{2,30},{3,31},{4,0},{5,1},{6,2},{7,3},{8,4},{9,5},{1... | collective-permute-start | bytes 98312 | tf_op jit(solution)/shard_map/ppermute | solution.py:38
  8.3 10.4 %collective-permute-start.4 = (bf16[64,256]{1,0:T(8,128)(2,1)S(1)}, bf16[64,256]{1,0:T(8,128)(2,1)S(1)}, u32[]{:S(2)}, u32[]{:S(2)}) collective-permute-start(bf16[64,256]{1,0:T(8,128)(2,1)S(1)} %get-tuple-element.45), channel_id=1, source_target_pairs={{0,29},{1,28},{2,31},{3,30},{4,1},{5,0},{6,3},{7,2},{8,5},{9,4},{1... | collective-permute-start | bytes 98312 | tf_op jit(solution)/shard_map/ppermute | solution.py:38
  9.1 2.2 %copy-start = (bf16[64,32768]{1,0:T(8,128)(2,1)S(1)}, bf16[64,32768]{1,0:T(8,128)(2,1)}, u32[]{:S(2)}) copy-start(bf16[64,32768]{1,0:T(8,128)(2,1)} %refs_0_.5) | copy-start | bytes 12582916
  11.3 7.9 %copy-start.6 = (bf16[64,4096]{1,0:T(8,128)(2,1)S(1)}, bf16[64,4096]{1,0:T(8,128)(2,1)}, u32[]{:S(2)}) copy-start(bf16[64,4096]{1,0:T(8,128)(2,1)} %refs_2_.1) | copy-start | bytes 1572868
  11.3 7.9 %copy-start.11 = (s32[4,1024]{1,0:T(4,128)S(1)}, s32[4,1024]{1,0:T(4,128)}, u32[]{:S(2)}) copy-start(s32[4,1024]{1,0:T(4,128)} %pick_ref.3) | copy-start | bytes 49156
  12.2 16.3 %copy-start.16 = (f32[4096]{0:T(1024)S(1)}, f32[4096]{0:T(1024)}, u32[]{:S(2)}) copy-start(f32[4096]{0:T(1024)} %param.8) | copy-start | bytes 49156
  12.2 16.3 %copy-start.17 = (f32[4096]{0:T(1024)S(1)}, f32[4096]{0:T(1024)}, u32[]{:S(2)}) copy-start(f32[4096]{0:T(1024)} %param.9) | copy-start | bytes 49156
  12.2 16.3 %copy-start.12 = (f32[1,1024]{1,0:T(1,128)S(1)}, f32[1,1024]{1,0:T(1,128)}, u32[]{:S(2)}) copy-start(f32[1,1024]{1,0:T(1,128)} %taper_ref.1) | copy-start | bytes 12292
  12.3 14.5 %collective-permute-start.5 = (f32[2,256]{1,0:T(2,128)S(1)}, f32[2,256]{1,0:T(2,128)S(1)}, u32[]{:S(2)}, u32[]{:S(2)}) collective-permute-start(f32[2,256]{1,0:T(2,128)S(1)} %get-tuple-element.48), channel_id=1, source_target_pairs={{0,4},{1,5},{2,6},{3,7},{4,8},{5,9},{6,10},{7,11},{8,12},{9,13},{1... | collective-permute-start | bytes 6152 | tf_op jit(solution)/shard_map/ppermute | solution.py:37
  13.9 14.6 %collective-permute-start.6 = (f32[2,256]{1,0:T(2,128)S(1)}, f32[2,256]{1,0:T(2,128)S(1)}, u32[]{:S(2)}, u32[]{:S(2)}) collective-permute-start(f32[2,256]{1,0:T(2,128)S(1)} %get-tuple-element.47), channel_id=1, source_target_pairs={{0,28},{1,29},{2,30},{3,31},{4,0},{5,1},{6,2},{7,3},{8,4},{9,5},{1... | collective-permute-start | bytes 6152 | tf_op jit(solution)/shard_map/ppermute | solution.py:38
  17.1 19.6 %collective-permute-start.15 = (bf16[64,4096]{1,0:T(8,128)(2,1)}, bf16[64,4096]{1,0:T(8,128)(2,1)S(1)}, u32[]{:S(2)}, u32[]{:S(2)}) collective-permute-start(bf16[64,4096]{1,0:T(8,128)(2,1)} %get-tuple-element.31), channel_id=1, source_target_pairs={{0,2},{1,3},{2,0},{3,1},{4,6},{5,7},{6,4},{7,5},{8,10},{9,11},{10,... | collective-permute-start | bytes 1572872 | tf_op jit(solution)/shard_map/ppermute | solution.py:30
  18.7 38.9 %collective-permute-start.16 = (bf16[64,4096]{1,0:T(8,128)(2,1)S(1)}, bf16[64,4096]{1,0:T(8,128)(2,1)S(1)}, u32[]{:S(2)}, u32[]{:S(2)}) collective-permute-start(bf16[64,4096]{1,0:T(8,128)(2,1)S(1)} %get-tuple-element.32), channel_id=1, source_target_pairs={{0,3},{1,2},{2,1},{3,0},{4,7},{5,6},{6,5},{7,4},{8,11},{9,10},{10,... | collective-permute-start | bytes 1572872 | tf_op jit(solution)/shard_map/ppermute | solution.py:30
  18.7 40.7 %collective-permute-start.14 = (bf16[64,4096]{1,0:T(8,128)(2,1)S(1)}, bf16[64,4096]{1,0:T(8,128)(2,1)S(1)}, u32[]{:S(2)}, u32[]{:S(2)}) collective-permute-start(bf16[64,4096]{1,0:T(8,128)(2,1)S(1)} %pack.10), channel_id=1, source_target_pairs={{0,1},{1,0},{2,3},{3,2},{4,5},{5,4},{6,7},{7,6},{8,9},{9,8},{10,11... | collective-permute-start | bytes 1572872 | tf_op jit(solution)/shard_map/ppermute | solution.py:30
  26.9 22.2 %collective-permute-start.7 = (bf16[1024,128]{1,0:T(8,128)(2,1)}, bf16[1024,128]{1,0:T(8,128)(2,1)}, u32[]{:S(2)}, u32[]{:S(2)}) collective-permute-start(bf16[1024,128]{1,0:T(8,128)(2,1)} %slice_bitcast_fusion), channel_id=1, source_target_pairs={{0,2},{1,3},{2,0},{3,1},{4,6},{5,7},{6,4},{7,5},{8,10},{9,11},{10,... | collective-permute-start | bytes 786440 | tf_op jit(solution)/shard_map/ppermute | solution.py:30
  33.0 2.2 %copy-start.1 = (bf16[64,32768]{1,0:T(8,128)(2,1)S(1)}, bf16[64,32768]{1,0:T(8,128)(2,1)}, u32[]{:S(2)}) copy-start(bf16[64,32768]{1,0:T(8,128)(2,1)} %refs_0_.5) | copy-start | bytes 12582916
  36.2 26.6 %collective-permute-start.12 = (bf16[64,2048]{1,0:T(8,128)(2,1)S(1)}, bf16[64,2048]{1,0:T(8,128)(2,1)S(1)}, u32[]{:S(2)}, u32[]{:S(2)}) collective-permute-start(bf16[64,2048]{1,0:T(8,128)(2,1)S(1)} %get-tuple-element.29), channel_id=1, source_target_pairs={{0,2},{1,3},{2,0},{3,1},{4,6},{5,7},{6,4},{7,5},{8,10},{9,11},{10,... | collective-permute-start | bytes 786440 | tf_op jit(solution)/shard_map/ppermute | solution.py:30
  36.7 23.1 %copy-start.2 = (bf16[64,32768]{1,0:T(8,128)(2,1)S(1)}, bf16[64,32768]{1,0:T(8,128)(2,1)}, u32[]{:S(2)}) copy-start(bf16[64,32768]{1,0:T(8,128)(2,1)} %refs_0_.5) | copy-start | bytes 12582916
  36.7 26.2 %collective-permute-start.13 = (bf16[64,2048]{1,0:T(8,128)(2,1)S(1)}, bf16[64,2048]{1,0:T(8,128)(2,1)S(1)}, u32[]{:S(2)}, u32[]{:S(2)}) collective-permute-start(bf16[64,2048]{1,0:T(8,128)(2,1)S(1)} %get-tuple-element.30), channel_id=1, source_target_pairs={{0,3},{1,2},{2,1},{3,0},{4,7},{5,6},{6,5},{7,4},{8,11},{9,10},{10,... | collective-permute-start | bytes 786440 | tf_op jit(solution)/shard_map/ppermute | solution.py:30
  49.1 16.1 %collective-permute-start.11 = (bf16[64,2048]{1,0:T(8,128)(2,1)S(1)}, bf16[64,2048]{1,0:T(8,128)(2,1)S(1)}, u32[]{:S(2)}, u32[]{:S(2)}) collective-permute-start(bf16[64,2048]{1,0:T(8,128)(2,1)S(1)} %pack.8), channel_id=1, source_target_pairs={{0,1},{1,0},{2,3},{3,2},{4,5},{5,4},{6,7},{7,6},{8,9},{9,8},{10,11... | collective-permute-start | bytes 786440 | tf_op jit(solution)/shard_map/ppermute | solution.py:30
  57.6 10.7 %collective-permute-start.10 = (bf16[64,2048]{1,0:T(8,128)(2,1)}, bf16[64,2048]{1,0:T(8,128)(2,1)S(1)}, u32[]{:S(2)}, u32[]{:S(2)}) collective-permute-start(bf16[64,2048]{1,0:T(8,128)(2,1)} %get-tuple-element.28), channel_id=1, source_target_pairs={{0,3},{1,2},{2,1},{3,0},{4,7},{5,6},{6,5},{7,4},{8,11},{9,10},{10,... | collective-permute-start | bytes 786440 | tf_op jit(solution)/shard_map/ppermute | solution.py:30
  59.4 15.3 %collective-permute-start.9 = (bf16[64,2048]{1,0:T(8,128)(2,1)}, bf16[64,2048]{1,0:T(8,128)(2,1)S(1)}, u32[]{:S(2)}, u32[]{:S(2)}) collective-permute-start(bf16[64,2048]{1,0:T(8,128)(2,1)} %get-tuple-element.27), channel_id=1, source_target_pairs={{0,2},{1,3},{2,0},{3,1},{4,6},{5,7},{6,4},{7,5},{8,10},{9,11},{10,... | collective-permute-start | bytes 786440 | tf_op jit(solution)/shard_map/ppermute | solution.py:30
  62.8 17.6 %collective-permute-start.17 = (bf16[64,4096]{1,0:T(8,128)(2,1)}, bf16[64,4096]{1,0:T(8,128)(2,1)S(1)}, u32[]{:S(2)}, u32[]{:S(2)}) collective-permute-start(bf16[64,4096]{1,0:T(8,128)(2,1)} %get-tuple-element.36), channel_id=1, source_target_pairs={{0,1},{1,0},{2,3},{3,2},{4,5},{5,4},{6,7},{7,6},{8,9},{9,8},{10,11... | collective-permute-start | bytes 1572872 | tf_op jit(solution)/shard_map/ppermute | solution.py:30
  62.8 0.7 copy-start.7
  63.5 20.5 %collective-permute-start.18 = (bf16[64,4096]{1,0:T(8,128)(2,1)}, bf16[64,4096]{1,0:T(8,128)(2,1)S(1)}, u32[]{:S(2)}, u32[]{:S(2)}) collective-permute-start(bf16[64,4096]{1,0:T(8,128)(2,1)} %get-tuple-element.37), channel_id=1, source_target_pairs={{0,2},{1,3},{2,0},{3,1},{4,6},{5,7},{6,4},{7,5},{8,10},{9,11},{10,... | collective-permute-start | bytes 1572872 | tf_op jit(solution)/shard_map/ppermute | solution.py:30
  65.1 0.7 copy-start.9
  65.9 28.6 %collective-permute-start.19 = (bf16[64,4096]{1,0:T(8,128)(2,1)}, bf16[64,4096]{1,0:T(8,128)(2,1)S(1)}, u32[]{:S(2)}, u32[]{:S(2)}) collective-permute-start(bf16[64,4096]{1,0:T(8,128)(2,1)} %get-tuple-element.38), channel_id=1, source_target_pairs={{0,3},{1,2},{2,1},{3,0},{4,7},{5,6},{6,5},{7,4},{8,11},{9,10},{10,... | collective-permute-start | bytes 1572872 | tf_op jit(solution)/shard_map/ppermute | solution.py:30
  66.1 2.2 %copy-start.3 = (bf16[64,32768]{1,0:T(8,128)(2,1)S(1)}, bf16[64,32768]{1,0:T(8,128)(2,1)}, u32[]{:S(2)}) copy-start(bf16[64,32768]{1,0:T(8,128)(2,1)} %refs_0_.5) | copy-start | bytes 12582916
  68.3 0.9 copy-start.8
  68.3 1.0 copy-start.10
  68.4 6.6 %collective-permute-start.8 = (bf16[64,2048]{1,0:T(8,128)(2,1)S(1)}, bf16[64,2048]{1,0:T(8,128)(2,1)S(1)}, u32[]{:S(2)}, u32[]{:S(2)}) collective-permute-start(bf16[64,2048]{1,0:T(8,128)(2,1)S(1)} %pack.6), channel_id=1, source_target_pairs={{0,1},{1,0},{2,3},{3,2},{4,5},{5,4},{6,7},{7,6},{8,9},{9,8},{10,11... | collective-permute-start | bytes 786440 | tf_op jit(solution)/shard_map/ppermute | solution.py:30
  69.3 2.2 %copy-start.4 = (bf16[64,32768]{1,0:T(8,128)(2,1)S(1)}, bf16[64,32768]{1,0:T(8,128)(2,1)}, u32[]{:S(2)}) copy-start(bf16[64,32768]{1,0:T(8,128)(2,1)} %refs_0_.5) | copy-start | bytes 12582916
  73.3 0.7 copy-start.13
  73.9 0.7 copy-start.15
  74.6 5.7 %collective-permute-start.20 = (bf16[64,2048]{1,0:T(8,128)(2,1)}, bf16[64,2048]{1,0:T(8,128)(2,1)S(1)}, u32[]{:S(2)}, u32[]{:S(2)}) collective-permute-start(bf16[64,2048]{1,0:T(8,128)(2,1)} %get-tuple-element.39), channel_id=1, source_target_pairs={{0,1},{1,0},{2,3},{3,2},{4,5},{5,4},{6,7},{7,6},{8,9},{9,8},{10,11... | collective-permute-start | bytes 786440 | tf_op jit(solution)/shard_map/ppermute | solution.py:30
  74.9 25.9 %collective-permute-start.21 = (bf16[64,2048]{1,0:T(8,128)(2,1)}, bf16[64,2048]{1,0:T(8,128)(2,1)S(1)}, u32[]{:S(2)}, u32[]{:S(2)}) collective-permute-start(bf16[64,2048]{1,0:T(8,128)(2,1)} %copy-done.15), channel_id=1, source_target_pairs={{0,2},{1,3},{2,0},{3,1},{4,6},{5,7},{6,4},{7,5},{8,10},{9,11},{10,... | collective-permute-start | bytes 786440 | tf_op jit(solution)/shard_map/ppermute | solution.py:30
  76.5 2.2 %copy-start.5 = (bf16[64,32768]{1,0:T(8,128)(2,1)S(1)}, bf16[64,32768]{1,0:T(8,128)(2,1)}, u32[]{:S(2)}) copy-start(bf16[64,32768]{1,0:T(8,128)(2,1)} %refs_0_.5) | copy-start | bytes 12582916
  78.7 1.7 %copy-start.14 = (bf16[64,2048]{1,0:T(8,128)(2,1)S(1)}, bf16[64,2048]{1,0:T(8,128)(2,1)}, u32[]{:S(2)}) copy-start(bf16[64,2048]{1,0:T(8,128)(2,1)} %copy-done.13) | copy-start | bytes 786436
  80.4 25.2 %collective-permute-start.22 = (bf16[64,2048]{1,0:T(8,128)(2,1)S(1)}, bf16[64,2048]{1,0:T(8,128)(2,1)S(1)}, u32[]{:S(2)}, u32[]{:S(2)}) collective-permute-start(bf16[64,2048]{1,0:T(8,128)(2,1)S(1)} %copy-done.14), channel_id=1, source_target_pairs={{0,3},{1,2},{2,1},{3,0},{4,7},{5,6},{6,5},{7,4},{8,11},{9,10},{10,... | collective-permute-start | bytes 786440 | tf_op jit(solution)/shard_map/ppermute | solution.py:30
  80.4 26.1 %collective-permute-start.23 = (bf16[64,2048]{1,0:T(8,128)(2,1)S(1)}, bf16[64,2048]{1,0:T(8,128)(2,1)S(1)}, u32[]{:S(2)}, u32[]{:S(2)}) collective-permute-start(bf16[64,2048]{1,0:T(8,128)(2,1)S(1)} %get-tuple-element.42), channel_id=1, source_target_pairs={{0,1},{1,0},{2,3},{3,2},{4,5},{5,4},{6,7},{7,6},{8,9},{9,8},{10,11... | collective-permute-start | bytes 786440 | tf_op jit(solution)/shard_map/ppermute | solution.py:30
  84.0 28.1 %collective-permute-start.24 = (bf16[64,2048]{1,0:T(8,128)(2,1)S(1)}, bf16[64,2048]{1,0:T(8,128)(2,1)S(1)}, u32[]{:S(2)}, u32[]{:S(2)}) collective-permute-start(bf16[64,2048]{1,0:T(8,128)(2,1)S(1)} %get-tuple-element.43), channel_id=1, source_target_pairs={{0,2},{1,3},{2,0},{3,1},{4,6},{5,7},{6,4},{7,5},{8,10},{9,11},{10,... | collective-permute-start | bytes 786440 | tf_op jit(solution)/shard_map/ppermute | solution.py:30
  94.5 21.9 %collective-permute-start.25 = (bf16[64,2048]{1,0:T(8,128)(2,1)S(1)}, bf16[64,2048]{1,0:T(8,128)(2,1)S(1)}, u32[]{:S(2)}, u32[]{:S(2)}) collective-permute-start(bf16[64,2048]{1,0:T(8,128)(2,1)S(1)} %get-tuple-element.44), channel_id=1, source_target_pairs={{0,3},{1,2},{2,1},{3,0},{4,7},{5,6},{6,5},{7,4},{8,11},{9,10},{10,... | collective-permute-start | bytes 786440 | tf_op jit(solution)/shard_map/ppermute | solution.py:30
